TPU v7x, 32 devices: a whole 2x2x4 slice. The times are simulated.
32 devices in a mesh: layer: 8 (over y, x, core), tile: 4 (over z).
Axes of the slice: x: 2, y: 2, z: 4, core: 2. Of those that a mesh axis runs over, the one named last changes fastest.
Arguments:
- incident: bfloat16 [4096, 128], P('tile'), may hold values from -6 to 6
- interface: bfloat16 [16, 4096, 4096], P('layer', 'tile'), may hold values from -0.09375 to 0.09375
- eigvec: bfloat16 [16, 4096, 4096], P('layer', 'tile'), may hold values from -0.09375 to 0.09375
- angle: float32 [16, 4096], P('layer'), may hold values from -3.140625 to 3.140625
- decay: float32 [16, 4096], P('layer'), may hold values from 0.002 to 0.15
Outputs:
- fields: bfloat16 [16, 4096, 512], P('layer', 'tile')
- leaving: float32 [16, 4096, 128], P('layer', 'tile')
All inputs are finite; a program needn't handle non-finite values.
Results may differ from a plain program's by a relative error of at most 0.035.
Values sent between devices are 32-bit elements; how exact they have to be, the bound alone decides.
A program may use at most 128 MiB of HBM per device.

v0:
```python
import jax
import jax.numpy as jnp
from jax import lax
from jax.sharding import PartitionSpec as P

DEPTHS = 4


def shifted(x, axis, by):
    peers = lax.axis_size(axis)
    pairs = [(i, i + by) for i in range(peers) if 0 <= i + by < peers]
    return lax.ppermute(x, axis, pairs)


def rotate(block, angle_row, decay_row, frac):
    half = block.shape[1] // 2
    real_part = block[:, :half]
    imag_part = block[:, half:]
    scale = jnp.exp(-frac * decay_row)
    cosine = (scale * jnp.cos(frac * angle_row))[:, None]
    sine = (scale * jnp.sin(frac * angle_row))[:, None]
    return jnp.concatenate(
        [cosine * real_part - sine * imag_part, sine * real_part + cosine * imag_part], axis=1
    )


def advance(current, interface, angle, decay):
    fulls = []
    leaves = []
    for layer_num in range(interface.shape[0]):
        full = lax.all_gather(current, "tile", axis=0, tiled=True)
        fulls.append(full)
        phased = rotate(full, angle[layer_num], decay[layer_num], 1.0).astype(jnp.bfloat16)
        current = jnp.dot(interface[layer_num], phased, preferred_element_type=jnp.float32)
        leaves.append(current)
    return (jnp.stack(fulls), jnp.stack(leaves))


def pick_block(values, block_num, block_width, half):
    real_part = lax.dynamic_slice_in_dim(
        values, block_num * block_width, block_width, values.ndim - 1
    )
    imag_part = lax.dynamic_slice_in_dim(
        values, half + block_num * block_width, block_width, values.ndim - 1
    )
    return jnp.concatenate([real_part, imag_part], axis=values.ndim - 1)


def put_block(values, piece, block_num, block_width, half):
    last = values.ndim - 1
    real_piece = lax.slice_in_dim(piece, 0, block_width, axis=last)
    imag_piece = lax.slice_in_dim(piece, block_width, 2 * block_width, axis=last)
    values = lax.dynamic_update_slice_in_dim(values, real_piece, block_num * block_width, last)
    return lax.dynamic_update_slice_in_dim(values, imag_piece, half + block_num * block_width, last)


def on_device(incident, interface, eigvec, angle, decay):
    groups = lax.axis_size("layer")
    member = lax.axis_index("layer")
    layers_here = interface.shape[0]
    shard_rows = interface.shape[1]
    orders = interface.shape[2]
    width = incident.shape[1]
    half = width // 2
    start_amps = incident.astype(jnp.float32)
    store_full = jnp.zeros((layers_here, orders, width), jnp.float32)
    store_leave = jnp.zeros((layers_here, shard_rows, width), jnp.float32)
    block_count = 4
    block_width = half // block_count
    inbox = jnp.zeros((shard_rows, 2 * block_width), jnp.float32)

    def step_blocks(step, carry):
        inbox, store_full, store_leave = carry
        block_num = step - member
        valid = (block_num >= 0) & (block_num < block_count)
        clipped = jnp.clip(block_num, 0, block_count - 1)
        source = jnp.where(member == 0, pick_block(start_amps, clipped, block_width, half), inbox)
        fulls, leaves = advance(source, interface, angle, decay)
        store_full = jnp.where(
            valid, put_block(store_full, fulls, clipped, block_width, half), store_full
        )
        store_leave = jnp.where(
            valid, put_block(store_leave, leaves, clipped, block_width, half), store_leave
        )
        inbox = shifted(leaves[layers_here - 1], "layer", 1)
        return (inbox, store_full, store_leave)

    inbox, store_full, store_leave = lax.fori_loop(
        0, groups + block_count - 1, step_blocks, (inbox, store_full, store_leave)
    )
    fields = []
    for layer_num in range(layers_here):
        depth = jnp.concatenate(
            [
                rotate(
                    store_full[layer_num], angle[layer_num], decay[layer_num], step / DEPTHS
                ).astype(jnp.bfloat16)
                for step in range(DEPTHS)
            ],
            axis=1,
        )
        fields.append(
            jnp.dot(eigvec[layer_num], depth, preferred_element_type=jnp.float32).astype(
                jnp.bfloat16
            )
        )
    return (jnp.stack(fields), store_leave)


def solution(mesh):
    in_specs = (
        P("tile", None),
        P("layer", "tile", None),
        P("layer", "tile", None),
        P("layer", None),
        P("layer", None),
    )
    out_specs = (P("layer", "tile", None), P("layer", "tile", None))
    return jax.shard_map(
        on_device, mesh=mesh, in_specs=in_specs, out_specs=out_specs, check_vma=False
    )
```

profile of v0, /device:TPU:1, one launch (start us, length us, event | category | flops | bytes accessed | tf_op | source)
XLA Modules:
  0.0 704.2 jit_solution(1159093125117101727)
XLA Ops:
  11.3 665.6 %while.20 = (s32[]{:T(128)}, f32[1024,32]{0,1:T(8,128)S(1)}, f32[2,4096,128]{1,2,0:T(8,128)}, f32[2,1024,128]{1,2,0:T(8,128)S(1)}, f32[2,4096]{1,0:T(2,128)}, /*...) while((s32[]{:T(128)}, f32[1024,32]{0,1:T(8,128)S(1)}, ...), condition=%wide.region_1.2_spmd.clone, body=%wide.region_0.1_spmd.clone.sunk | while | flops 543318016 | bytes 56263120 | solution.py:88
  12.3 15.3 %all_gather.24 = f32[4096,32]{0,1:T(8,128)S(1)} all-gather(f32[1024,32]{0,1:T(8,128)S(1)} %maximum_select_fusion.2), channel_id=1, replica_groups=mesh['layer'=8,'tile'=4] {'tile'}, dimensions={0}, use_global_device_ids=true | all-gather | bytes 655360 | tf_op jit(solution)/shard_map/while/body/eval_jaxpr/all_gather | solution.py:31
  34.4 11.9 %all_gather.25 = f32[4096,32]{0,1:T(8,128)S(1)} all-gather(f32[1024,32]{0,1:T(8,128)S(1)} %bitcast.104), channel_id=1, replica_groups=mesh['layer'=8,'tile'=4] {'tile'}, dimensions={0}, use_global_device_ids=true | all-gather | bytes 655360 | tf_op jit(solution)/shard_map/while/body/eval_jaxpr/all_gather | solution.py:31
  53.0 9.5 %collective-permute-start = (f32[1024,32]{0,1:T(8,128)S(1)}, f32[1024,32]{0,1:T(8,128)S(1)}, u32[]{:S(2)}, u32[]{:S(2)}) collective-permute-start(f32[1024,32]{0,1:T(8,128)S(1)} %bitcast.107), channel_id=1, source_target_pairs={{0,4},{4,8},{8,12},{12,16},{16,20},{20,24},{24,28},{1,5},{5,9},{9,... | collective-permute-start | bytes 393224 | tf_op jit(solution)/shard_map/while/body/eval_jaxpr/ppermute | solution.py:12
  71.0 13.6 %all_gather.24 = f32[4096,32]{0,1:T(8,128)S(1)} all-gather(f32[1024,32]{0,1:T(8,128)S(1)} %maximum_select_fusion.2), channel_id=1, replica_groups=mesh['layer'=8,'tile'=4] {'tile'}, dimensions={0}, use_global_device_ids=true | all-gather | bytes 655360 | tf_op jit(solution)/shard_map/while/body/eval_jaxpr/all_gather | solution.py:31
  91.3 11.9 %all_gather.25 = f32[4096,32]{0,1:T(8,128)S(1)} all-gather(f32[1024,32]{0,1:T(8,128)S(1)} %bitcast.104), channel_id=1, replica_groups=mesh['layer'=8,'tile'=4] {'tile'}, dimensions={0}, use_global_device_ids=true | all-gather | bytes 655360 | tf_op jit(solution)/shard_map/while/body/eval_jaxpr/all_gather | solution.py:31
  132.1 14.9 %all_gather.24 = f32[4096,32]{0,1:T(8,128)S(1)} all-gather(f32[1024,32]{0,1:T(8,128)S(1)} %maximum_select_fusion.2), channel_id=1, replica_groups=mesh['layer'=8,'tile'=4] {'tile'}, dimensions={0}, use_global_device_ids=true | all-gather | bytes 655360 | tf_op jit(solution)/shard_map/while/body/eval_jaxpr/all_gather | solution.py:31
  153.7 14.3 %all_gather.25 = f32[4096,32]{0,1:T(8,128)S(1)} all-gather(f32[1024,32]{0,1:T(8,128)S(1)} %bitcast.104), channel_id=1, replica_groups=mesh['layer'=8,'tile'=4] {'tile'}, dimensions={0}, use_global_device_ids=true | all-gather | bytes 655360 | tf_op jit(solution)/shard_map/while/body/eval_jaxpr/all_gather | solution.py:31
  193.1 15.5 %all_gather.24 = f32[4096,32]{0,1:T(8,128)S(1)} all-gather(f32[1024,32]{0,1:T(8,128)S(1)} %maximum_select_fusion.2), channel_id=1, replica_groups=mesh['layer'=8,'tile'=4] {'tile'}, dimensions={0}, use_global_device_ids=true | all-gather | bytes 655360 | tf_op jit(solution)/shard_map/while/body/eval_jaxpr/all_gather | solution.py:31
  215.4 13.9 %all_gather.25 = f32[4096,32]{0,1:T(8,128)S(1)} all-gather(f32[1024,32]{0,1:T(8,128)S(1)} %bitcast.104), channel_id=1, replica_groups=mesh['layer'=8,'tile'=4] {'tile'}, dimensions={0}, use_global_device_ids=true | all-gather | bytes 655360 | tf_op jit(solution)/shard_map/while/body/eval_jaxpr/all_gather | solution.py:31
  255.2 14.3 %all_gather.24 = f32[4096,32]{0,1:T(8,128)S(1)} all-gather(f32[1024,32]{0,1:T(8,128)S(1)} %maximum_select_fusion.2), channel_id=1, replica_groups=mesh['layer'=8,'tile'=4] {'tile'}, dimensions={0}, use_global_device_ids=true | all-gather | bytes 655360 | tf_op jit(solution)/shard_map/while/body/eval_jaxpr/all_gather | solution.py:31
  276.2 13.6 %all_gather.25 = f32[4096,32]{0,1:T(8,128)S(1)} all-gather(f32[1024,32]{0,1:T(8,128)S(1)} %bitcast.104), channel_id=1, replica_groups=mesh['layer'=8,'tile'=4] {'tile'}, dimensions={0}, use_global_device_ids=true | all-gather | bytes 655360 | tf_op jit(solution)/shard_map/while/body/eval_jaxpr/all_gather | solution.py:31
  316.4 14.3 %all_gather.24 = f32[4096,32]{0,1:T(8,128)S(1)} all-gather(f32[1024,32]{0,1:T(8,128)S(1)} %maximum_select_fusion.2), channel_id=1, replica_groups=mesh['layer'=8,'tile'=4] {'tile'}, dimensions={0}, use_global_device_ids=true | all-gather | bytes 655360 | tf_op jit(solution)/shard_map/while/body/eval_jaxpr/all_gather | solution.py:31
  337.4 13.9 %all_gather.25 = f32[4096,32]{0,1:T(8,128)S(1)} all-gather(f32[1024,32]{0,1:T(8,128)S(1)} %bitcast.104), channel_id=1, replica_groups=mesh['layer'=8,'tile'=4] {'tile'}, dimensions={0}, use_global_device_ids=true | all-gather | bytes 655360 | tf_op jit(solution)/shard_map/while/body/eval_jaxpr/all_gather | solution.py:31
  376.7 13.5 %all_gather.24 = f32[4096,32]{0,1:T(8,128)S(1)} all-gather(f32[1024,32]{0,1:T(8,128)S(1)} %maximum_select_fusion.2), channel_id=1, replica_groups=mesh['layer'=8,'tile'=4] {'tile'}, dimensions={0}, use_global_device_ids=true | all-gather | bytes 655360 | tf_op jit(solution)/shard_map/while/body/eval_jaxpr/all_gather | solution.py:31
  397.0 13.6 %all_gather.25 = f32[4096,32]{0,1:T(8,128)S(1)} all-gather(f32[1024,32]{0,1:T(8,128)S(1)} %bitcast.104), channel_id=1, replica_groups=mesh['layer'=8,'tile'=4] {'tile'}, dimensions={0}, use_global_device_ids=true | all-gather | bytes 655360 | tf_op jit(solution)/shard_map/while/body/eval_jaxpr/all_gather | solution.py:31
  438.2 12.0 %all_gather.24 = f32[4096,32]{0,1:T(8,128)S(1)} all-gather(f32[1024,32]{0,1:T(8,128)S(1)} %maximum_select_fusion.2), channel_id=1, replica_groups=mesh['layer'=8,'tile'=4] {'tile'}, dimensions={0}, use_global_device_ids=true | all-gather | bytes 655360 | tf_op jit(solution)/shard_map/while/body/eval_jaxpr/all_gather | solution.py:31
  456.9 14.2 %all_gather.25 = f32[4096,32]{0,1:T(8,128)S(1)} all-gather(f32[1024,32]{0,1:T(8,128)S(1)} %bitcast.104), channel_id=1, replica_groups=mesh['layer'=8,'tile'=4] {'tile'}, dimensions={0}, use_global_device_ids=true | all-gather | bytes 655360 | tf_op jit(solution)/shard_map/while/body/eval_jaxpr/all_gather | solution.py:31
  498.2 12.1 %all_gather.24 = f32[4096,32]{0,1:T(8,128)S(1)} all-gather(f32[1024,32]{0,1:T(8,128)S(1)} %maximum_select_fusion.2), channel_id=1, replica_groups=mesh['layer'=8,'tile'=4] {'tile'}, dimensions={0}, use_global_device_ids=true | all-gather | bytes 655360 | tf_op jit(solution)/shard_map/while/body/eval_jaxpr/all_gather | solution.py:31
  517.0 14.0 %all_gather.25 = f32[4096,32]{0,1:T(8,128)S(1)} all-gather(f32[1024,32]{0,1:T(8,128)S(1)} %bitcast.104), channel_id=1, replica_groups=mesh['layer'=8,'tile'=4] {'tile'}, dimensions={0}, use_global_device_ids=true | all-gather | bytes 655360 | tf_op jit(solution)/shard_map/while/body/eval_jaxpr/all_gather | solution.py:31
  558.0 12.3 %all_gather.24 = f32[4096,32]{0,1:T(8,128)S(1)} all-gather(f32[1024,32]{0,1:T(8,128)S(1)} %maximum_select_fusion.2), channel_id=1, replica_groups=mesh['layer'=8,'tile'=4] {'tile'}, dimensions={0}, use_global_device_ids=true | all-gather | bytes 655360 | tf_op jit(solution)/shard_map/while/body/eval_jaxpr/all_gather | solution.py:31
  577.1 13.9 %all_gather.25 = f32[4096,32]{0,1:T(8,128)S(1)} all-gather(f32[1024,32]{0,1:T(8,128)S(1)} %bitcast.104), channel_id=1, replica_groups=mesh['layer'=8,'tile'=4] {'tile'}, dimensions={0}, use_global_device_ids=true | all-gather | bytes 655360 | tf_op jit(solution)/shard_map/while/body/eval_jaxpr/all_gather | solution.py:31
  617.9 12.3 %all_gather.24 = f32[4096,32]{0,1:T(8,128)S(1)} all-gather(f32[1024,32]{0,1:T(8,128)S(1)} %maximum_select_fusion.2), channel_id=1, replica_groups=mesh['layer'=8,'tile'=4] {'tile'}, dimensions={0}, use_global_device_ids=true | all-gather | bytes 655360 | tf_op jit(solution)/shard_map/while/body/eval_jaxpr/all_gather | solution.py:31
  636.9 14.3 %all_gather.25 = f32[4096,32]{0,1:T(8,128)S(1)} all-gather(f32[1024,32]{0,1:T(8,128)S(1)} %bitcast.104), channel_id=1, replica_groups=mesh['layer'=8,'tile'=4] {'tile'}, dimensions={0}, use_global_device_ids=true | all-gather | bytes 655360 | tf_op jit(solution)/shard_map/while/body/eval_jaxpr/all_gather | solution.py:31
  (314 shorter events, 392.6 us)
Async XLA Ops:
  53.0 16.9 %collective-permute-start = (f32[1024,32]{0,1:T(8,128)S(1)}, f32[1024,32]{0,1:T(8,128)S(1)}, u32[]{:S(2)}, u32[]{:S(2)}) collective-permute-start(f32[1024,32]{0,1:T(8,128)S(1)} %bitcast.107), channel_id=1, source_target_pairs={{0,4},{4,8},{8,12},{12,16},{16,20},{20,24},{24,28},{1,5},{5,9},{9,... | collective-permute-start | bytes 393224 | tf_op jit(solution)/shard_map/while/body/eval_jaxpr/ppermute | solution.py:12
  109.9 21.1 %collective-permute-start = (f32[1024,32]{0,1:T(8,128)S(1)}, f32[1024,32]{0,1:T(8,128)S(1)}, u32[]{:S(2)}, u32[]{:S(2)}) collective-permute-start(f32[1024,32]{0,1:T(8,128)S(1)} %bitcast.107), channel_id=1, source_target_pairs={{0,4},{4,8},{8,12},{12,16},{16,20},{20,24},{24,28},{1,5},{5,9},{9,... | collective-permute-start | bytes 393224 | tf_op jit(solution)/shard_map/while/body/eval_jaxpr/ppermute | solution.py:12
  124.4 6.6 copy-start.2
  174.8 17.3 %collective-permute-start = (f32[1024,32]{0,1:T(8,128)S(1)}, f32[1024,32]{0,1:T(8,128)S(1)}, u32[]{:S(2)}, u32[]{:S(2)}) collective-permute-start(f32[1024,32]{0,1:T(8,128)S(1)} %bitcast.107), channel_id=1, source_target_pairs={{0,4},{4,8},{8,12},{12,16},{16,20},{20,24},{24,28},{1,5},{5,9},{9,... | collective-permute-start | bytes 393224 | tf_op jit(solution)/shard_map/while/body/eval_jaxpr/ppermute | solution.py:12
  185.5 6.6 copy-start.2
  236.1 18.1 %collective-permute-start = (f32[1024,32]{0,1:T(8,128)S(1)}, f32[1024,32]{0,1:T(8,128)S(1)}, u32[]{:S(2)}, u32[]{:S(2)}) collective-permute-start(f32[1024,32]{0,1:T(8,128)S(1)} %bitcast.107), channel_id=1, source_target_pairs={{0,4},{4,8},{8,12},{12,16},{16,20},{20,24},{24,28},{1,5},{5,9},{9,... | collective-permute-start | bytes 393224 | tf_op jit(solution)/shard_map/while/body/eval_jaxpr/ppermute | solution.py:12
  247.6 6.6 copy-start.2
  296.6 18.7 %collective-permute-start = (f32[1024,32]{0,1:T(8,128)S(1)}, f32[1024,32]{0,1:T(8,128)S(1)}, u32[]{:S(2)}, u32[]{:S(2)}) collective-permute-start(f32[1024,32]{0,1:T(8,128)S(1)} %bitcast.107), channel_id=1, source_target_pairs={{0,4},{4,8},{8,12},{12,16},{16,20},{20,24},{24,28},{1,5},{5,9},{9,... | collective-permute-start | bytes 393224 | tf_op jit(solution)/shard_map/while/body/eval_jaxpr/ppermute | solution.py:12
  308.7 6.6 copy-start.2
  358.0 17.6 %collective-permute-start = (f32[1024,32]{0,1:T(8,128)S(1)}, f32[1024,32]{0,1:T(8,128)S(1)}, u32[]{:S(2)}, u32[]{:S(2)}) collective-permute-start(f32[1024,32]{0,1:T(8,128)S(1)} %bitcast.107), channel_id=1, source_target_pairs={{0,4},{4,8},{8,12},{12,16},{16,20},{20,24},{24,28},{1,5},{5,9},{9,... | collective-permute-start | bytes 393224 | tf_op jit(solution)/shard_map/while/body/eval_jaxpr/ppermute | solution.py:12
  370.3 5.3 copy-start.2
  417.3 19.8 %collective-permute-start = (f32[1024,32]{0,1:T(8,128)S(1)}, f32[1024,32]{0,1:T(8,128)S(1)}, u32[]{:S(2)}, u32[]{:S(2)}) collective-permute-start(f32[1024,32]{0,1:T(8,128)S(1)} %bitcast.107), channel_id=1, source_target_pairs={{0,4},{4,8},{8,12},{12,16},{16,20},{20,24},{24,28},{1,5},{5,9},{9,... | collective-permute-start | bytes 393224 | tf_op jit(solution)/shard_map/while/body/eval_jaxpr/ppermute | solution.py:12
  431.8 5.3 copy-start.2
  477.9 19.2 %collective-permute-start = (f32[1024,32]{0,1:T(8,128)S(1)}, f32[1024,32]{0,1:T(8,128)S(1)}, u32[]{:S(2)}, u32[]{:S(2)}) collective-permute-start(f32[1024,32]{0,1:T(8,128)S(1)} %bitcast.107), channel_id=1, source_target_pairs={{0,4},{4,8},{8,12},{12,16},{16,20},{20,24},{24,28},{1,5},{5,9},{9,... | collective-permute-start | bytes 393224 | tf_op jit(solution)/shard_map/while/body/eval_jaxpr/ppermute | solution.py:12
  491.8 5.3 copy-start.2
  537.8 19.1 %collective-permute-start = (f32[1024,32]{0,1:T(8,128)S(1)}, f32[1024,32]{0,1:T(8,128)S(1)}, u32[]{:S(2)}, u32[]{:S(2)}) collective-permute-start(f32[1024,32]{0,1:T(8,128)S(1)} %bitcast.107), channel_id=1, source_target_pairs={{0,4},{4,8},{8,12},{12,16},{16,20},{20,24},{24,28},{1,5},{5,9},{9,... | collective-permute-start | bytes 393224 | tf_op jit(solution)/shard_map/while/body/eval_jaxpr/ppermute | solution.py:12
  551.6 5.3 copy-start.2
  597.8 19.1 %collective-permute-start = (f32[1024,32]{0,1:T(8,128)S(1)}, f32[1024,32]{0,1:T(8,128)S(1)}, u32[]{:S(2)}, u32[]{:S(2)}) collective-permute-start(f32[1024,32]{0,1:T(8,128)S(1)} %bitcast.107), channel_id=1, source_target_pairs={{0,4},{4,8},{8,12},{12,16},{16,20},{20,24},{24,28},{1,5},{5,9},{9,... | collective-permute-start | bytes 393224 | tf_op jit(solution)/shard_map/while/body/eval_jaxpr/ppermute | solution.py:12
  611.6 5.3 copy-start.2
  658.0 18.9 %collective-permute-start = (f32[1024,32]{0,1:T(8,128)S(1)}, f32[1024,32]{0,1:T(8,128)S(1)}, u32[]{:S(2)}, u32[]{:S(2)}) collective-permute-start(f32[1024,32]{0,1:T(8,128)S(1)} %bitcast.107), channel_id=1, source_target_pairs={{0,4},{4,8},{8,12},{12,16},{16,20},{20,24},{24,28},{1,5},{5,9},{9,... | collective-permute-start | bytes 393224 | tf_op jit(solution)/shard_map/while/body/eval_jaxpr/ppermute | solution.py:12
  671.5 5.3 copy-start.2
  676.9 5.3 copy-start.15
  685.7 7.5 %copy-start.4 = (f32[1,4096]{1,0:T(1,128)S(1)}, f32[1,4096]{1,0:T(1,128)}, u32[]{:S(2)}) copy-start(f32[1,4096]{1,0:T(1,128)} %get-tuple-element.339) | copy-start | bytes 49156
  685.7 7.5 %copy-start.8 = (f32[1,4096]{1,0:T(1,128)S(1)}, f32[1,4096]{1,0:T(1,128)}, u32[]{:S(2)}) copy-start(f32[1,4096]{1,0:T(1,128)} %get-tuple-element.344) | copy-start | bytes 49156
  (26 other events, 42.6 us)
where the time goes:
time: 709 us; the launch traced here: 704 us
  blocking collectives  300 us (42%)
  other arithmetic  173 us (24%)
  matrix products  145 us (20%)
  starting transfers between devices  74.1 us (10%)
  local copies, waits for them, and re-layouts  9.94 us (1%)
    all_gather x22, blocking collectives, advance(): full = lax.all_gather(current, 'tile', axis=0, tiled=True)  300 us
    dot_general x22, matrix products, advance(): jnp.dot(interface[layer_num], phased, preferred_element_type=jnp.float32)  131 us
    ppermute x11, starting transfers between devices, shifted(): return lax.ppermute(x, axis, pairs)  74.1 us
    select_n x11, other arithmetic, step_blocks(): jnp.where(valid, put_block(store_full, fulls, clipped, block_width, half)...  57.7 us
    while x22, other arithmetic  50.2 us
    mul x24, other arithmetic, rotate(): cosine = (scale * jnp.cos(frac * angle_row))[:, None]  25.5 us
    dot_general x2, matrix products, on_device(): jnp.dot(eigvec[layer_num], depth, preferred_element_type=jnp.float32)  14.4 us
  transfers between devices with their start and end apart: 11, of which 0 were waited for; matrix products, arithmetic and copies ran while one was open for 19% of the time, Pallas kernels for 0%

commit v1 on v0

--- a/solution.py
+++ b/solution.py
@@ -28,7 +28,13 @@
     fulls = []
     leaves = []
     for layer_num in range(interface.shape[0]):
-        full = lax.all_gather(current, "tile", axis=0, tiled=True)
+
+        def store_the_seats_all(vector):
+            z2 = jnp.stack(jax.lax.axis_size("tile") * [vector], axis=0)
+            h_now = jax.lax.all_to_all(z2, axis_name="tile", split_axis=0, concat_axis=0)
+            return jnp.concatenate(h_now, 0)
+
+        full = store_the_seats_all(current)
         fulls.append(full)
         phased = rotate(full, angle[layer_num], decay[layer_num], 1.0).astype(jnp.bfloat16)
         current = jnp.dot(interface[layer_num], phased, preferred_element_type=jnp.float32)

time: 709 us -> 758 us (1.069)
  blocking collectives: 300 us -> 0 us
  waiting for transfers between devices: 0.03 us -> 206 us
  local copies, waits for them, and re-layouts: 9.94 us -> 146 us
  starting transfers between devices: 74.1 us -> 106 us
  other arithmetic: 173 us -> 145 us
    all_gather x22 -> x0, blocking collectives: 300 us -> none  [advance(): full = lax.all_gather(current, 'tile', axis=0, tiled=True)]
    all_to_all x0 -> x22, waiting for transfers between devices: none -> 206 us  [store_the_seats_all(): jax.lax.all_to_all(z2, axis_name='tile', split_axis=0, concat_axis=0)]
    all_to_all x0 -> x22, starting transfers between devices: none -> 78.3 us  [store_the_seats_all(): jax.lax.all_to_all(z2, axis_name='tile', split_axis=0, concat_axis=0)]
    ppermute x11, starting transfers between devices: 74.1 us -> 27.4 us  [shifted(): return lax.ppermute(x, axis, pairs)]
    dynamic_update_slice x0 -> x22, local copies, waits for them, and re-layouts: none -> 41.6 us  [the longest x11 20.8 us: put_block(): lax.dynamic_update_slice_in_dim(values, real_piece, block_num * block_wid...]
    reshape x0 -> x44, local copies, waits for them, and re-layouts: none -> 31.7 us  [the longest x22 30.8 us: advance(): return (jnp.stack(fulls), jnp.stack(leaves))]
    another operation x0 -> x33, local copies, waits for them, and re-layouts: none -> 28.3 us  [the longest x22 19.1 us: store_the_seats_all(): z2 = jnp.stack(jax.lax.axis_size('tile') * [vector], axis=0)]
    all_to_all x0 -> x22, local copies, waits for them, and re-layouts: none -> 25 us  [store_the_seats_all(): jax.lax.all_to_all(z2, axis_name='tile', split_axis=0, concat_axis=0)]
  transfers between devices with their start and end apart: 11 -> 33, of which waited for: 0 -> 22; matrix products, arithmetic and copies ran while one was open for 19% -> 33% of each run, Pallas kernels for 0% -> 0%
where the time goes in v1:
time: 758 us; the launch traced here: 751 us
  waiting for transfers between devices  206 us (27%)
  local copies, waits for them, and re-layouts  146 us (19%)
  other arithmetic  145 us (19%)
  matrix products  145 us (19%)
  starting transfers between devices  106 us (14%)
    all_to_all x22, waiting for transfers between devices, store_the_seats_all(): jax.lax.all_to_all(z2, axis_name='tile', split_axis=0, concat_axis=0)  206 us
    dot_general x22, matrix products, advance(): jnp.dot(interface[layer_num], phased, preferred_element_type=jnp.float32)  131 us
    all_to_all x22, starting transfers between devices, store_the_seats_all(): jax.lax.all_to_all(z2, axis_name='tile', split_axis=0, concat_axis=0)  78.3 us
    select_n x11, other arithmetic, step_blocks(): jnp.where(valid, put_block(store_full, fulls, clipped, block_width, half)...  58.6 us
    while x22, other arithmetic  49.5 us
    reshape x22, local copies, waits for them, and re-layouts, advance(): return (jnp.stack(fulls), jnp.stack(leaves))  30.8 us
    ppermute x11, starting transfers between devices, shifted(): return lax.ppermute(x, axis, pairs)  27.4 us
    all_to_all x22, local copies, waits for them, and re-layouts, store_the_seats_all(): jax.lax.all_to_all(z2, axis_name='tile', split_axis=0, concat_axis=0)  25 us
  transfers between devices with their start and end apart: 33, of which 22 were waited for; matrix products, arithmetic and copies ran while one was open for 33% of the time, Pallas kernels for 0%

profile of v1, /device:TPU:1, one launch (start us, length us, event | category | flops | bytes accessed | tf_op | source)
XLA Modules:
  0.0 751.1 jit_solution(8185279228357362888)
XLA Ops:
  11.2 712.4 %while.20 = (s32[]{:T(128)}, f32[1024,32]{0,1:T(8,128)S(1)}, f32[2,4096,128]{1,2,0:T(8,128)}, f32[2,1024,128]{1,2,0:T(8,128)S(1)}, f32[2,4096]{1,0:T(2,128)}, /*...) while((s32[]{:T(128)}, f32[1024,32]{0,1:T(8,128)S(1)}, ...), condition=%wide.region_1.2_spmd.clone, body=%wide.region_0.1_spmd.clone.sunk | while | flops 543055872 | bytes 66880072 | solution.py:94
  21.0 10.7 %all-to-all-done = f32[4,1024,32]{1,2,0:T(8,128)S(1)} async-done(((f32[4,1024,32]{1,2,0:T(8,128)}), f32[4,1024,32]{1,2,0:T(8,128)S(1)}, u32[]{:S(2)}, u32[]{:S(2)}) %all-to-all-start) | async-done | bytes 524320 | tf_op jit(solution)/shard_map/while/body/eval_jaxpr/all_to_all | solution.py:34
  46.3 9.8 %all-to-all-done.1 = f32[4,1024,32]{1,2,0:T(8,128)S(1)} async-done(((f32[4,1024,32]{1,2,0:T(8,128)}), f32[4,1024,32]{1,2,0:T(8,128)S(1)}, u32[]{:S(2)}, u32[]{:S(2)}) %all-to-all-start.1) | async-done | bytes 524320 | tf_op jit(solution)/shard_map/while/body/eval_jaxpr/all_to_all | solution.py:34
  87.0 8.5 %all-to-all-done = f32[4,1024,32]{1,2,0:T(8,128)S(1)} async-done(((f32[4,1024,32]{1,2,0:T(8,128)}), f32[4,1024,32]{1,2,0:T(8,128)S(1)}, u32[]{:S(2)}, u32[]{:S(2)}) %all-to-all-start) | async-done | bytes 524320 | tf_op jit(solution)/shard_map/while/body/eval_jaxpr/all_to_all | solution.py:34
  110.2 9.8 %all-to-all-done.1 = f32[4,1024,32]{1,2,0:T(8,128)S(1)} async-done(((f32[4,1024,32]{1,2,0:T(8,128)}), f32[4,1024,32]{1,2,0:T(8,128)S(1)}, u32[]{:S(2)}, u32[]{:S(2)}) %all-to-all-start.1) | async-done | bytes 524320 | tf_op jit(solution)/shard_map/while/body/eval_jaxpr/all_to_all | solution.py:34
  154.4 7.9 %all-to-all-done = f32[4,1024,32]{1,2,0:T(8,128)S(1)} async-done(((f32[4,1024,32]{1,2,0:T(8,128)}), f32[4,1024,32]{1,2,0:T(8,128)S(1)}, u32[]{:S(2)}, u32[]{:S(2)}) %all-to-all-start) | async-done | bytes 524320 | tf_op jit(solution)/shard_map/while/body/eval_jaxpr/all_to_all | solution.py:34
  176.9 10.6 %all-to-all-done.1 = f32[4,1024,32]{1,2,0:T(8,128)S(1)} async-done(((f32[4,1024,32]{1,2,0:T(8,128)}), f32[4,1024,32]{1,2,0:T(8,128)S(1)}, u32[]{:S(2)}, u32[]{:S(2)}) %all-to-all-start.1) | async-done | bytes 524320 | tf_op jit(solution)/shard_map/while/body/eval_jaxpr/all_to_all | solution.py:34
  220.5 9.2 %all-to-all-done = f32[4,1024,32]{1,2,0:T(8,128)S(1)} async-done(((f32[4,1024,32]{1,2,0:T(8,128)}), f32[4,1024,32]{1,2,0:T(8,128)S(1)}, u32[]{:S(2)}, u32[]{:S(2)}) %all-to-all-start) | async-done | bytes 524320 | tf_op jit(solution)/shard_map/while/body/eval_jaxpr/all_to_all | solution.py:34
  244.3 9.9 %all-to-all-done.1 = f32[4,1024,32]{1,2,0:T(8,128)S(1)} async-done(((f32[4,1024,32]{1,2,0:T(8,128)}), f32[4,1024,32]{1,2,0:T(8,128)S(1)}, u32[]{:S(2)}, u32[]{:S(2)}) %all-to-all-start.1) | async-done | bytes 524320 | tf_op jit(solution)/shard_map/while/body/eval_jaxpr/all_to_all | solution.py:34
  286.1 8.5 %all-to-all-done = f32[4,1024,32]{1,2,0:T(8,128)S(1)} async-done(((f32[4,1024,32]{1,2,0:T(8,128)}), f32[4,1024,32]{1,2,0:T(8,128)S(1)}, u32[]{:S(2)}, u32[]{:S(2)}) %all-to-all-start) | async-done | bytes 524320 | tf_op jit(solution)/shard_map/while/body/eval_jaxpr/all_to_all | solution.py:34
  309.2 9.8 %all-to-all-done.1 = f32[4,1024,32]{1,2,0:T(8,128)S(1)} async-done(((f32[4,1024,32]{1,2,0:T(8,128)}), f32[4,1024,32]{1,2,0:T(8,128)S(1)}, u32[]{:S(2)}, u32[]{:S(2)}) %all-to-all-start.1) | async-done | bytes 524320 | tf_op jit(solution)/shard_map/while/body/eval_jaxpr/all_to_all | solution.py:34
  350.9 9.5 %all-to-all-done = f32[4,1024,32]{1,2,0:T(8,128)S(1)} async-done(((f32[4,1024,32]{1,2,0:T(8,128)}), f32[4,1024,32]{1,2,0:T(8,128)S(1)}, u32[]{:S(2)}, u32[]{:S(2)}) %all-to-all-start) | async-done | bytes 524320 | tf_op jit(solution)/shard_map/while/body/eval_jaxpr/all_to_all | solution.py:34
  375.0 9.9 %all-to-all-done.1 = f32[4,1024,32]{1,2,0:T(8,128)S(1)} async-done(((f32[4,1024,32]{1,2,0:T(8,128)}), f32[4,1024,32]{1,2,0:T(8,128)S(1)}, u32[]{:S(2)}, u32[]{:S(2)}) %all-to-all-start.1) | async-done | bytes 524320 | tf_op jit(solution)/shard_map/while/body/eval_jaxpr/all_to_all | solution.py:34
  415.6 8.5 %all-to-all-done = f32[4,1024,32]{1,2,0:T(8,128)S(1)} async-done(((f32[4,1024,32]{1,2,0:T(8,128)}), f32[4,1024,32]{1,2,0:T(8,128)S(1)}, u32[]{:S(2)}, u32[]{:S(2)}) %all-to-all-start) | async-done | bytes 524320 | tf_op jit(solution)/shard_map/while/body/eval_jaxpr/all_to_all | solution.py:34
  438.8 9.8 %all-to-all-done.1 = f32[4,1024,32]{1,2,0:T(8,128)S(1)} async-done(((f32[4,1024,32]{1,2,0:T(8,128)}), f32[4,1024,32]{1,2,0:T(8,128)S(1)}, u32[]{:S(2)}, u32[]{:S(2)}) %all-to-all-start.1) | async-done | bytes 524320 | tf_op jit(solution)/shard_map/while/body/eval_jaxpr/all_to_all | solution.py:34
  479.2 8.5 %all-to-all-done = f32[4,1024,32]{1,2,0:T(8,128)S(1)} async-done(((f32[4,1024,32]{1,2,0:T(8,128)}), f32[4,1024,32]{1,2,0:T(8,128)S(1)}, u32[]{:S(2)}, u32[]{:S(2)}) %all-to-all-start) | async-done | bytes 524320 | tf_op jit(solution)/shard_map/while/body/eval_jaxpr/all_to_all | solution.py:34
  502.3 9.8 %all-to-all-done.1 = f32[4,1024,32]{1,2,0:T(8,128)S(1)} async-done(((f32[4,1024,32]{1,2,0:T(8,128)}), f32[4,1024,32]{1,2,0:T(8,128)S(1)}, u32[]{:S(2)}, u32[]{:S(2)}) %all-to-all-start.1) | async-done | bytes 524320 | tf_op jit(solution)/shard_map/while/body/eval_jaxpr/all_to_all | solution.py:34
  542.8 8.5 %all-to-all-done = f32[4,1024,32]{1,2,0:T(8,128)S(1)} async-done(((f32[4,1024,32]{1,2,0:T(8,128)}), f32[4,1024,32]{1,2,0:T(8,128)S(1)}, u32[]{:S(2)}, u32[]{:S(2)}) %all-to-all-start) | async-done | bytes 524320 | tf_op jit(solution)/shard_map/while/body/eval_jaxpr/all_to_all | solution.py:34
  566.0 9.8 %all-to-all-done.1 = f32[4,1024,32]{1,2,0:T(8,128)S(1)} async-done(((f32[4,1024,32]{1,2,0:T(8,128)}), f32[4,1024,32]{1,2,0:T(8,128)S(1)}, u32[]{:S(2)}, u32[]{:S(2)}) %all-to-all-start.1) | async-done | bytes 524320 | tf_op jit(solution)/shard_map/while/body/eval_jaxpr/all_to_all | solution.py:34
  606.4 8.5 %all-to-all-done = f32[4,1024,32]{1,2,0:T(8,128)S(1)} async-done(((f32[4,1024,32]{1,2,0:T(8,128)}), f32[4,1024,32]{1,2,0:T(8,128)S(1)}, u32[]{:S(2)}, u32[]{:S(2)}) %all-to-all-start) | async-done | bytes 524320 | tf_op jit(solution)/shard_map/while/body/eval_jaxpr/all_to_all | solution.py:34
  629.6 9.8 %all-to-all-done.1 = f32[4,1024,32]{1,2,0:T(8,128)S(1)} async-done(((f32[4,1024,32]{1,2,0:T(8,128)}), f32[4,1024,32]{1,2,0:T(8,128)S(1)}, u32[]{:S(2)}, u32[]{:S(2)}) %all-to-all-start.1) | async-done | bytes 524320 | tf_op jit(solution)/shard_map/while/body/eval_jaxpr/all_to_all | solution.py:34
  670.0 8.5 %all-to-all-done = f32[4,1024,32]{1,2,0:T(8,128)S(1)} async-done(((f32[4,1024,32]{1,2,0:T(8,128)}), f32[4,1024,32]{1,2,0:T(8,128)S(1)}, u32[]{:S(2)}, u32[]{:S(2)}) %all-to-all-start) | async-done | bytes 524320 | tf_op jit(solution)/shard_map/while/body/eval_jaxpr/all_to_all | solution.py:34
  693.2 9.8 %all-to-all-done.1 = f32[4,1024,32]{1,2,0:T(8,128)S(1)} async-done(((f32[4,1024,32]{1,2,0:T(8,128)}), f32[4,1024,32]{1,2,0:T(8,128)S(1)}, u32[]{:S(2)}, u32[]{:S(2)}) %all-to-all-start.1) | async-done | bytes 524320 | tf_op jit(solution)/shard_map/while/body/eval_jaxpr/all_to_all | solution.py:34
  732.6 7.3 fusion.32
  (490 shorter events, 535.0 us)
Async XLA Ops:
  12.2 19.5 %all-to-all-start = ((f32[4,1024,32]{1,2,0:T(8,128)}), f32[4,1024,32]{1,2,0:T(8,128)S(1)}, u32[]{:S(2)}, u32[]{:S(2)}) async-start(f32[4,1024,32]{1,2,0:T(8,128)} %stack.80), calls=%async_computation | async-start | bytes 1048576 | tf_op jit(solution)/shard_map/while/body/eval_jaxpr/all_to_all | solution.py:34
  38.6 17.5 %all-to-all-start.1 = ((f32[4,1024,32]{1,2,0:T(8,128)}), f32[4,1024,32]{1,2,0:T(8,128)S(1)}, u32[]{:S(2)}, u32[]{:S(2)}) async-start(f32[4,1024,32]{1,2,0:T(8,128)} %stack.81), calls=%async_computation.1 | async-start | bytes 1048576 | tf_op jit(solution)/shard_map/while/body/eval_jaxpr/all_to_all | solution.py:34
  78.0 17.5 %all-to-all-start = ((f32[4,1024,32]{1,2,0:T(8,128)}), f32[4,1024,32]{1,2,0:T(8,128)S(1)}, u32[]{:S(2)}, u32[]{:S(2)}) async-start(f32[4,1024,32]{1,2,0:T(8,128)} %stack.80), calls=%async_computation | async-start | bytes 1048576 | tf_op jit(solution)/shard_map/while/body/eval_jaxpr/all_to_all | solution.py:34
  102.5 17.5 %all-to-all-start.1 = ((f32[4,1024,32]{1,2,0:T(8,128)}), f32[4,1024,32]{1,2,0:T(8,128)S(1)}, u32[]{:S(2)}, u32[]{:S(2)}) async-start(f32[4,1024,32]{1,2,0:T(8,128)} %stack.81), calls=%async_computation.1 | async-start | bytes 1048576 | tf_op jit(solution)/shard_map/while/body/eval_jaxpr/all_to_all | solution.py:34
  126.0 18.4 %collective-permute-start = (f32[1024,32]{0,1:T(8,128)S(1)}, f32[1024,32]{0,1:T(8,128)S(1)}, u32[]{:S(2)}, u32[]{:S(2)}) collective-permute-start(f32[1024,32]{0,1:T(8,128)S(1)} %bitcast.117), channel_id=1, source_target_pairs={{0,4},{4,8},{8,12},{12,16},{16,20},{20,24},{24,28},{1,5},{5,9},{9,... | collective-permute-start | bytes 393224 | tf_op jit(solution)/shard_map/while/body/eval_jaxpr/ppermute | solution.py:12
  145.4 16.9 %all-to-all-start = ((f32[4,1024,32]{1,2,0:T(8,128)}), f32[4,1024,32]{1,2,0:T(8,128)S(1)}, u32[]{:S(2)}, u32[]{:S(2)}) async-start(f32[4,1024,32]{1,2,0:T(8,128)} %stack.80), calls=%async_computation | async-start | bytes 1048576 | tf_op jit(solution)/shard_map/while/body/eval_jaxpr/all_to_all | solution.py:34
  169.2 18.3 %all-to-all-start.1 = ((f32[4,1024,32]{1,2,0:T(8,128)}), f32[4,1024,32]{1,2,0:T(8,128)S(1)}, u32[]{:S(2)}, u32[]{:S(2)}) async-start(f32[4,1024,32]{1,2,0:T(8,128)} %stack.81), calls=%async_computation.1 | async-start | bytes 1048576 | tf_op jit(solution)/shard_map/while/body/eval_jaxpr/all_to_all | solution.py:34
  193.6 16.9 %collective-permute-start = (f32[1024,32]{0,1:T(8,128)S(1)}, f32[1024,32]{0,1:T(8,128)S(1)}, u32[]{:S(2)}, u32[]{:S(2)}) collective-permute-start(f32[1024,32]{0,1:T(8,128)S(1)} %bitcast.117), channel_id=1, source_target_pairs={{0,4},{4,8},{8,12},{12,16},{16,20},{20,24},{24,28},{1,5},{5,9},{9,... | collective-permute-start | bytes 393224 | tf_op jit(solution)/shard_map/while/body/eval_jaxpr/ppermute | solution.py:12
  211.5 18.2 %all-to-all-start = ((f32[4,1024,32]{1,2,0:T(8,128)}), f32[4,1024,32]{1,2,0:T(8,128)S(1)}, u32[]{:S(2)}, u32[]{:S(2)}) async-start(f32[4,1024,32]{1,2,0:T(8,128)} %stack.80), calls=%async_computation | async-start | bytes 1048576 | tf_op jit(solution)/shard_map/while/body/eval_jaxpr/all_to_all | solution.py:34
  236.6 17.6 %all-to-all-start.1 = ((f32[4,1024,32]{1,2,0:T(8,128)}), f32[4,1024,32]{1,2,0:T(8,128)S(1)}, u32[]{:S(2)}, u32[]{:S(2)}) async-start(f32[4,1024,32]{1,2,0:T(8,128)} %stack.81), calls=%async_computation.1 | async-start | bytes 1048576 | tf_op jit(solution)/shard_map/while/body/eval_jaxpr/all_to_all | solution.py:34
  277.1 17.5 %all-to-all-start = ((f32[4,1024,32]{1,2,0:T(8,128)}), f32[4,1024,32]{1,2,0:T(8,128)S(1)}, u32[]{:S(2)}, u32[]{:S(2)}) async-start(f32[4,1024,32]{1,2,0:T(8,128)} %stack.80), calls=%async_computation | async-start | bytes 1048576 | tf_op jit(solution)/shard_map/while/body/eval_jaxpr/all_to_all | solution.py:34
  301.5 17.5 %all-to-all-start.1 = ((f32[4,1024,32]{1,2,0:T(8,128)}), f32[4,1024,32]{1,2,0:T(8,128)S(1)}, u32[]{:S(2)}, u32[]{:S(2)}) async-start(f32[4,1024,32]{1,2,0:T(8,128)} %stack.81), calls=%async_computation.1 | async-start | bytes 1048576 | tf_op jit(solution)/shard_map/while/body/eval_jaxpr/all_to_all | solution.py:34
  341.9 18.4 %all-to-all-start = ((f32[4,1024,32]{1,2,0:T(8,128)}), f32[4,1024,32]{1,2,0:T(8,128)S(1)}, u32[]{:S(2)}, u32[]{:S(2)}) async-start(f32[4,1024,32]{1,2,0:T(8,128)} %stack.80), calls=%async_computation | async-start | bytes 1048576 | tf_op jit(solution)/shard_map/while/body/eval_jaxpr/all_to_all | solution.py:34
  367.3 17.6 %all-to-all-start.1 = ((f32[4,1024,32]{1,2,0:T(8,128)}), f32[4,1024,32]{1,2,0:T(8,128)S(1)}, u32[]{:S(2)}, u32[]{:S(2)}) async-start(f32[4,1024,32]{1,2,0:T(8,128)} %stack.81), calls=%async_computation.1 | async-start | bytes 1048576 | tf_op jit(solution)/shard_map/while/body/eval_jaxpr/all_to_all | solution.py:34
  406.6 17.5 %all-to-all-start = ((f32[4,1024,32]{1,2,0:T(8,128)}), f32[4,1024,32]{1,2,0:T(8,128)S(1)}, u32[]{:S(2)}, u32[]{:S(2)}) async-start(f32[4,1024,32]{1,2,0:T(8,128)} %stack.80), calls=%async_computation | async-start | bytes 1048576 | tf_op jit(solution)/shard_map/while/body/eval_jaxpr/all_to_all | solution.py:34
  431.1 17.5 %all-to-all-start.1 = ((f32[4,1024,32]{1,2,0:T(8,128)}), f32[4,1024,32]{1,2,0:T(8,128)S(1)}, u32[]{:S(2)}, u32[]{:S(2)}) async-start(f32[4,1024,32]{1,2,0:T(8,128)} %stack.81), calls=%async_computation.1 | async-start | bytes 1048576 | tf_op jit(solution)/shard_map/while/body/eval_jaxpr/all_to_all | solution.py:34
  470.2 17.5 %all-to-all-start = ((f32[4,1024,32]{1,2,0:T(8,128)}), f32[4,1024,32]{1,2,0:T(8,128)S(1)}, u32[]{:S(2)}, u32[]{:S(2)}) async-start(f32[4,1024,32]{1,2,0:T(8,128)} %stack.80), calls=%async_computation | async-start | bytes 1048576 | tf_op jit(solution)/shard_map/while/body/eval_jaxpr/all_to_all | solution.py:34
  494.6 17.5 %all-to-all-start.1 = ((f32[4,1024,32]{1,2,0:T(8,128)}), f32[4,1024,32]{1,2,0:T(8,128)S(1)}, u32[]{:S(2)}, u32[]{:S(2)}) async-start(f32[4,1024,32]{1,2,0:T(8,128)} %stack.81), calls=%async_computation.1 | async-start | bytes 1048576 | tf_op jit(solution)/shard_map/while/body/eval_jaxpr/all_to_all | solution.py:34
  533.9 17.5 %all-to-all-start = ((f32[4,1024,32]{1,2,0:T(8,128)}), f32[4,1024,32]{1,2,0:T(8,128)S(1)}, u32[]{:S(2)}, u32[]{:S(2)}) async-start(f32[4,1024,32]{1,2,0:T(8,128)} %stack.80), calls=%async_computation | async-start | bytes 1048576 | tf_op jit(solution)/shard_map/while/body/eval_jaxpr/all_to_all | solution.py:34
  558.3 17.5 %all-to-all-start.1 = ((f32[4,1024,32]{1,2,0:T(8,128)}), f32[4,1024,32]{1,2,0:T(8,128)S(1)}, u32[]{:S(2)}, u32[]{:S(2)}) async-start(f32[4,1024,32]{1,2,0:T(8,128)} %stack.81), calls=%async_computation.1 | async-start | bytes 1048576 | tf_op jit(solution)/shard_map/while/body/eval_jaxpr/all_to_all | solution.py:34
  597.4 17.5 %all-to-all-start = ((f32[4,1024,32]{1,2,0:T(8,128)}), f32[4,1024,32]{1,2,0:T(8,128)S(1)}, u32[]{:S(2)}, u32[]{:S(2)}) async-start(f32[4,1024,32]{1,2,0:T(8,128)} %stack.80), calls=%async_computation | async-start | bytes 1048576 | tf_op jit(solution)/shard_map/while/body/eval_jaxpr/all_to_all | solution.py:34
  621.9 17.5 %all-to-all-start.1 = ((f32[4,1024,32]{1,2,0:T(8,128)}), f32[4,1024,32]{1,2,0:T(8,128)S(1)}, u32[]{:S(2)}, u32[]{:S(2)}) async-start(f32[4,1024,32]{1,2,0:T(8,128)} %stack.81), calls=%async_computation.1 | async-start | bytes 1048576 | tf_op jit(solution)/shard_map/while/body/eval_jaxpr/all_to_all | solution.py:34
  661.0 17.5 %all-to-all-start = ((f32[4,1024,32]{1,2,0:T(8,128)}), f32[4,1024,32]{1,2,0:T(8,128)S(1)}, u32[]{:S(2)}, u32[]{:S(2)}) async-start(f32[4,1024,32]{1,2,0:T(8,128)} %stack.80), calls=%async_computation | async-start | bytes 1048576 | tf_op jit(solution)/shard_map/while/body/eval_jaxpr/all_to_all | solution.py:34
  685.4 17.5 %all-to-all-start.1 = ((f32[4,1024,32]{1,2,0:T(8,128)}), f32[4,1024,32]{1,2,0:T(8,128)S(1)}, u32[]{:S(2)}, u32[]{:S(2)}) async-start(f32[4,1024,32]{1,2,0:T(8,128)} %stack.81), calls=%async_computation.1 | async-start | bytes 1048576 | tf_op jit(solution)/shard_map/while/body/eval_jaxpr/all_to_all | solution.py:34
  (70 other events, 427.6 us)
